TPU v7x, 1024 devices: a whole 4x8x16 slice. The times are simulated.
1024 devices in a mesh: section: 16 (over z), dp: 32 (over y_lo, x, core), space: 2 (over y_hi).
Axes of the slice: x: 4, y: 8 (y_hi: 2, y_lo: 4; y = y_hi * 4 + y_lo), z: 16, core: 2. Of those that a mesh axis runs over, the one named last changes fastest.
Arguments:
- inputs: bfloat16 [16, 2, 32, 2, 8, 8, 256], P('section', None, 'dp', 'space'), may hold values from -6 to 6
- preacts: bfloat16 [16, 2, 32, 2, 8, 8, 256], P('section', None, 'dp', 'space'), may hold values from -6 to 6
- out_grad: bfloat16 [2, 32, 2, 8, 8, 256], P(None, 'dp', 'space'), may hold values from -6 to 6
- conv_w: bfloat16 [16, 27, 256, 256], P('section'), may hold values from -0.078125 to 0.078125
- proj_w: bfloat16 [16, 256, 256], P('section'), may hold values from -0.1875 to 0.1875
Outputs:
- section_grads: bfloat16 [16, 2, 32, 2, 8, 8, 256], P('section', None, 'dp', 'space')
- grad_conv: float32 [16, 256, 27, 256], P('section', 'dp')
- grad_proj: float32 [16, 256, 256], P('section', 'dp')
All inputs are finite; a program needn't handle non-finite values.
Results may differ from a plain program's by a relative error of at most 0.029.
Values may be sent and summed in bfloat16 or wider, within the bound.
A program may use at most 32 MiB of HBM per device.

v0:
```python
import jax
import jax.numpy as jnp
from jax import lax
from jax.sharding import PartitionSpec as P


def extended(cells, sides, width):
    for axis, dim in sides:
        count = lax.axis_size(axis)
        ends = count - 1
        head = lax.slice_in_dim(cells, 0, width, axis=dim)
        tail = lax.slice_in_dim(cells, cells.shape[dim] - width, cells.shape[dim], axis=dim)
        cells = jnp.concatenate(
            [
                lax.ppermute(tail, axis, [(i, (i + 1) % count) for i in range(ends)]),
                cells,
                lax.ppermute(head, axis, [((i + 1) % count, i) for i in range(ends)]),
            ],
            axis=dim,
        )
    return cells


def passed_along(block, axis, distance):
    devices = range(lax.axis_size(axis))
    route = [(i - distance, i) for i in devices if i - distance in devices]
    return lax.ppermute(block, axis, route)


def tap_offsets():
    return [
        (depth_off, row_off, col_off)
        for depth_off in (-1, 0, 1)
        for row_off in (-1, 0, 1)
        for col_off in (-1, 0, 1)
    ]


def shards(inputs, preacts, out_grad, conv_w, proj_w):
    section_count = lax.axis_size("section")
    section_id = lax.axis_index("section")
    micro_count = inputs.shape[1]
    depth_dev = inputs.shape[3]
    height = inputs.shape[4]
    plane_width = inputs.shape[5]
    channels = inputs.shape[6]
    row_count = depth_dev * height * plane_width
    scale_term = 1.0 / (micro_count * lax.axis_size("dp"))
    offsets = tap_offsets()
    tap_count = len(offsets)
    acts = inputs[0, :, 0]
    pre_acts = preacts[0, :, 0]
    seeds = out_grad[:, 0]
    conv_weight = conv_w[0]
    proj_weight = proj_w[0]
    acts_rim = extended(acts, (("space", 1),), 1)
    acts_ext = jnp.pad(acts_rim, ((0, 0), (0, 0), (1, 1), (1, 1), (0, 0)))
    hidden_all = jnp.maximum(pre_acts, jnp.zeros((), jnp.bfloat16)).reshape(
        micro_count, row_count, channels
    )
    contract_rows = (((0,), (0,)), ((), ()))
    contract_cols = (((1,), (1,)), ((), ()))
    grad_keep_init = jnp.zeros((micro_count, row_count, channels), jnp.bfloat16)
    seed_keep_init = jnp.zeros((micro_count, row_count, channels), jnp.bfloat16)
    outgoing_init = jnp.zeros((depth_dev, height, plane_width, channels), jnp.bfloat16)
    section_init = jnp.zeros((micro_count, depth_dev, height, plane_width, channels), jnp.bfloat16)

    def advance(step_index, carry):
        outgoing, section_out, grad_keep, seed_keep = carry
        incoming = passed_along(outgoing, "section", -1)
        micro_index = step_index - (section_count - 1 - section_id)
        active = (micro_index >= 0) & (micro_index < micro_count)
        safe_index = jnp.clip(micro_index, 0, micro_count - 1)
        seed_now = lax.dynamic_index_in_dim(seeds, safe_index, 0, keepdims=False)
        grad_out = jnp.where(section_id == section_count - 1, seed_now, incoming)
        grad_out_flat = grad_out.reshape(row_count, channels)
        pre_now = lax.dynamic_index_in_dim(pre_acts, safe_index, 0, keepdims=False).reshape(
            row_count, channels
        )

        def open_branch():
            grad_hidden = lax.dot_general(
                grad_out_flat, proj_weight, contract_cols, preferred_element_type=jnp.float32
            )
            masked = jnp.where(pre_now > 0, grad_hidden, jnp.zeros((), jnp.float32))
            return masked.astype(jnp.bfloat16).reshape(depth_dev, height, plane_width, channels)

        def skip_open():
            return jnp.zeros((depth_dev, height, plane_width, channels), jnp.bfloat16)

        grad_pre = lax.cond(active, open_branch, skip_open)
        grad_rim = extended(grad_pre, (("space", 0),), 1)
        grad_ext = jnp.pad(grad_rim, ((0, 0), (1, 1), (1, 1), (0, 0)))
        grad_flat = grad_pre.reshape(row_count, channels)

        def close_branch():
            total = grad_out_flat.astype(jnp.float32)
            for index, (depth_off, row_off, col_off) in enumerate(offsets):
                moved = grad_ext[
                    1 - depth_off : 1 - depth_off + depth_dev,
                    1 - row_off : 1 - row_off + height,
                    1 - col_off : 1 - col_off + plane_width,
                ]
                total = total + lax.dot_general(
                    moved.reshape(row_count, channels),
                    conv_weight[index],
                    contract_cols,
                    preferred_element_type=jnp.float32,
                )
            grad_in = total.astype(jnp.bfloat16).reshape(depth_dev, height, plane_width, channels)
            new_out = lax.dynamic_update_index_in_dim(section_out, grad_in, safe_index, 0)
            new_grad_keep = lax.dynamic_update_index_in_dim(grad_keep, grad_flat, safe_index, 0)
            new_seed_keep = lax.dynamic_update_index_in_dim(seed_keep, grad_out_flat, safe_index, 0)
            return (grad_in, new_out, new_grad_keep, new_seed_keep)

        def skip_close():
            return (jnp.zeros_like(outgoing), section_out, grad_keep, seed_keep)

        return lax.cond(active, close_branch, skip_close)

    init = (outgoing_init, section_init, grad_keep_init, seed_keep_init)
    final = lax.fori_loop(0, section_count + micro_count - 1, advance, init)
    section_out = final[1]
    grad_keep = final[2].reshape(micro_count * row_count, channels)
    seed_keep = final[3].reshape(micro_count * row_count, channels)
    shard_rows = channels // lax.axis_size("dp")
    columns = []
    for depth_off, row_off, col_off in offsets:
        columns.append(
            acts_ext[
                :,
                1 + depth_off : 1 + depth_off + depth_dev,
                1 + row_off : 1 + row_off + height,
                1 + col_off : 1 + col_off + plane_width,
            ]
        )
    unfolded = jnp.stack(columns, axis=-1).reshape(micro_count * row_count, channels * tap_count)
    conv_full = (
        lax.dot_general(unfolded, grad_keep, contract_rows, preferred_element_type=jnp.float32)
        * scale_term
    )
    conv_full = conv_full.reshape(channels, tap_count * channels)
    proj_full = (
        lax.dot_general(
            hidden_all.reshape(micro_count * row_count, channels),
            seed_keep,
            contract_rows,
            preferred_element_type=jnp.float32,
        )
        * scale_term
    )
    conv_shard, proj_shard = (
        lax.psum_scatter(
            conv_full.astype(jnp.bfloat16), "dp", scatter_dimension=0, tiled=True
        ).astype(jnp.float32),
        lax.psum_scatter(
            proj_full.astype(jnp.bfloat16), "dp", scatter_dimension=0, tiled=True
        ).astype(jnp.float32),
    )
    conv_sum, proj_sum = (
        lax.psum(conv_shard.astype(jnp.bfloat16), "space").astype(jnp.float32),
        lax.psum(proj_shard.astype(jnp.bfloat16), "space").astype(jnp.float32),
    )
    grad_conv = conv_sum.reshape(shard_rows, tap_count, channels)[None]
    grad_proj = proj_sum[None]
    section_grads = section_out[None, :, None]
    return (section_grads, grad_conv, grad_proj)


def solution(mesh):
    placed = (
        P("section", None, "dp", "space", None, None, None),
        P("section", None, "dp", "space", None, None, None),
        P(None, "dp", "space", None, None, None),
        P("section", None, None, None),
        P("section", None, None),
    )
    return jax.shard_map(
        shards,
        mesh=mesh,
        in_specs=placed,
        out_specs=(
            P("section", None, "dp", "space", None, None, None),
            P("section", "dp", None, None),
            P("section", "dp", None),
        ),
        check_vma=False,
    )
```

profile of v0, /device:TPU:1, one launch (start us, length us, event | category | flops | bytes accessed | tf_op | source)
XLA Modules:
  0.0 1047.5 jit_solution(13003903986821319886)
XLA Ops:
  7.2 8.3 collective-permute-start.3
  17.1 7.6 collective-permute-done.4
  26.4 6.3 copy.8
  32.7 11.8 %reshape.172 = bf16[128,6912]{1,0:T(8,128)(2,1)} reshape(bf16[2,1,8,8,256,27]{5,4,3,2,0,1:T(8,128)(2,1)} %copy.8) | data formatting | bytes 3538944 | tf_op jit(solution)/shard_map/reshape | solution.py:137
  45.1 592.7 %while.21 = (s32[]{:T(128)}, bf16[1,8,8,256]{3,2,1,0:T(8,128)(2,1)}, bf16[2,1,8,8,256]{4,3,2,1,0:T(8,128)(2,1)S(1)}, bf16[2,64,256]{2,1,0:T(8,128)(2,1)S(1)}, bf...) while((s32[]{:T(128)}, ...), condition=%wide.region_5.6_spmd, body=%wide.region_0.5_spmd.sunk | while | flops 235520000 | bytes 24773168 | solution.py:122
  52.6 7.9 collective-permute-start.2
  70.9 7.9 collective-permute-start.2
  88.7 7.9 collective-permute-start.2
  100.6 5.4 collective-permute-done
  108.0 7.9 collective-permute-start.2
  126.6 7.9 collective-permute-start.2
  138.5 5.1 collective-permute-done
  145.5 7.9 collective-permute-start.2
  164.1 7.9 collective-permute-start.2
  182.8 7.9 collective-permute-start.2
  201.4 7.9 collective-permute-start.2
  220.1 7.9 collective-permute-start.2
  238.6 7.9 collective-permute-start.2
  257.3 7.9 collective-permute-start.2
  275.9 7.9 collective-permute-start.2
  294.5 7.9 collective-permute-start.2
  306.4 5.1 collective-permute-done
  313.5 7.9 collective-permute-start.2
  325.4 246.7 %collective-permute-done = bf16[1,8,8,256]{3,2,1,0:T(8,128)(2,1)S(1)} collective-permute-done((bf16[1,8,8,256]{3,2,1,0:T(8,128)(2,1)}, bf16[1,8,8,256]{3,2,1,0:T(8,128)(2,1)S(1)}, u32[]{:S(2)}, u32[]{:S(2)}) %collective-permute-start) | collective-permute-done | bytes 32800 | tf_op jit(solution)/shard_map/while/body/eval_jaxpr/ppermute | solution.py:27
  575.0 7.9 collective-permute-start.2
  585.0 16.8 %conditional.5 = (bf16[1,8,8,256]{3,2,1,0:T(8,128)(2,1)}, bf16[2,1,8,8,256]{4,3,2,1,0:T(8,128)(2,1)S(1)}, bf16[2,64,256]{2,1,0:T(8,128)(2,1)S(1)}, bf16[2,64,256]{2,1,0:T(8,128)(2,1)S(1)}) conditional(s32[]{:T(128)} %convert_element_type.57, (bf16[2,1,8,8,256]{4,3,2,1,0:T(8,128)(2,1)S(1)}, bf16[2,64,256]{2,1,0:T(8,128)(2,1)S(1)}, ...), branch_computations={%region_3.3_spmd, %region_4.4_spmd} | conditional | flops 226967552 | bytes 23789670 | solution.py:119
  611.0 7.9 collective-permute-start.2
  621.0 16.8 %conditional.5 = (bf16[1,8,8,256]{3,2,1,0:T(8,128)(2,1)}, bf16[2,1,8,8,256]{4,3,2,1,0:T(8,128)(2,1)S(1)}, bf16[2,64,256]{2,1,0:T(8,128)(2,1)S(1)}, bf16[2,64,256]{2,1,0:T(8,128)(2,1)S(1)}) conditional(s32[]{:T(128)} %convert_element_type.57, (bf16[2,1,8,8,256]{4,3,2,1,0:T(8,128)(2,1)S(1)}, bf16[2,64,256]{2,1,0:T(8,128)(2,1)S(1)}, ...), branch_computations={%region_3.3_spmd, %region_4.4_spmd} | conditional | flops 226967552 | bytes 23789670 | solution.py:119
  647.8 181.1 %reduce-scatter.3.cloned.1.call-done = bf16[8,6912]{1,0:T(8,128)(2,1)} async-done(((bf16[256,6912]{1,0:T(8,128)(2,1)}), bf16[8,6912]{1,0:T(8,128)(2,1)}) %reduce-scatter.3.cloned.1.call-update) | async-done | bytes 110608 | tf_op jit(solution)/shard_map/reduce_scatter | solution.py:153
  828.8 154.7 %reduce-scatter.5.cloned.1.call-done = bf16[8,256]{1,0:T(8,128)(2,1)} async-done(((bf16[256,256]{1,0:T(8,128)(2,1)}), bf16[8,256]{1,0:T(8,128)(2,1)}) %reduce-scatter.5.cloned.1.call-update) | async-done | bytes 4112 | tf_op jit(solution)/shard_map/reduce_scatter | solution.py:156
  983.5 7.8 psum.15
  991.9 47.5 %all-reduce.4.cloned.1.call-done = bf16[1,8,27,256]{3,1,2,0:T(8,128)(2,1)} async-done(((bf16[1,8,27,256]{3,1,2,0:T(8,128)(2,1)}), bf16[1,8,27,256]{3,1,2,0:T(8,128)(2,1)}) %all-reduce.4.cloned.1.call-update) | async-done | bytes 110608 | tf_op jit(solution)/shard_map/psum | solution.py:161
  (320 shorter events, 232.9 us)
Async XLA Ops:
  7.2 821.6 %reduce-scatter.3.cloned.1.call-start = ((), (), s32[]{:S(2)}) async-start(), calls=%async_computation.2 | async-start | bytes 3649536 | tf_op jit(solution)/shard_map/reduce_scatter | solution.py:153
  7.2 9.9 collective-permute-start.3
  15.5 9.2 collective-permute-start.4
  51.3 9.2 collective-permute-start.1
  52.6 9.2 collective-permute-start.2
  69.6 9.2 collective-permute-start.1
  70.9 9.2 collective-permute-start.2
  87.4 9.2 collective-permute-start.1
  88.7 9.2 collective-permute-start.2
  106.7 9.2 collective-permute-start.1
  108.0 9.2 collective-permute-start.2
  125.3 9.2 collective-permute-start.1
  126.6 9.2 collective-permute-start.2
  144.2 9.2 collective-permute-start.1
  145.5 9.2 collective-permute-start.2
  162.8 9.2 collective-permute-start.1
  164.1 9.2 collective-permute-start.2
  181.5 9.2 collective-permute-start.1
  182.8 9.2 collective-permute-start.2
  201.4 9.4 collective-permute-start.2
  218.8 9.2 collective-permute-start.1
  220.1 9.2 collective-permute-start.2
  238.6 9.2 collective-permute-start.2
  257.3 9.2 collective-permute-start.2
  275.9 9.2 collective-permute-start.2
  294.5 9.2 collective-permute-start.2
  313.5 9.2 collective-permute-start.2
  324.1 248.0 %collective-permute-start = (bf16[1,8,8,256]{3,2,1,0:T(8,128)(2,1)}, bf16[1,8,8,256]{3,2,1,0:T(8,128)(2,1)S(1)}, u32[]{:S(2)}, u32[]{:S(2)}) collective-permute-start(bf16[1,8,8,256]{3,2,1,0:T(8,128)(2,1)} %get-tuple-element.500), channel_id=1, source_target_pairs={{64,0},{128,64},{192,128},{256,192},{320,256},{384,320},{448,384},... | collective-permute-start | bytes 98312 | tf_op jit(solution)/shard_map/while/body/eval_jaxpr/ppermute | solution.py:27
  575.0 9.2 collective-permute-start.2
  611.0 9.2 collective-permute-start.2
  646.0 337.5 %reduce-scatter.5.cloned.1.call-start = ((), (), s32[]{:S(2)}) async-start(), calls=%async_computation.4 | async-start | bytes 135168 | tf_op jit(solution)/shard_map/reduce_scatter | solution.py:156
  647.7 391.7 %all-reduce.4.cloned.1.call-start = ((), (), s32[]{:S(2)}) async-start(), calls=%async_computation.3 | async-start | bytes 221184 | tf_op jit(solution)/shard_map/psum | solution.py:161
  (35 other events, 254.5 us)
Sparse Core Ops, SparseCore 0:
  646.1 182.6 reduce-scatter.2
  832.8 150.7 reduce-scatter.4
  986.9 52.4 all-reduce.3
where the time goes:
time: 1050 us
  waiting for transfers between devices  736 us (70%)
  starting transfers between devices  187 us (18%)
  local copies, waits for them, and re-layouts  45.7 us (4%)
  matrix products  38.5 us (4%)
  other arithmetic  16.4 us (2%)
  between operations  14.1 us (1%)
    ppermute x17, waiting for transfers between devices, passed_along(): return lax.ppermute(block, axis, route)  323 us
    reduce_scatter x1, waiting for transfers between devices, shards(): lax.psum_scatter(conv_full.astype(jnp.bfloat16), 'dp', scatter_dimension=...  181 us
    reduce_scatter x1, waiting for transfers between devices, shards(): lax.psum_scatter(proj_full.astype(jnp.bfloat16), 'dp', scatter_dimension=...  155 us
    ppermute x18, starting transfers between devices, extended(): lax.ppermute(tail, axis, [(i, (i + 1) % count) for i in range(ends)])  142 us
    psum x1, waiting for transfers between devices, shards(): lax.psum(conv_shard.astype(jnp.bfloat16), 'space').astype(jnp.float32)  47.5 us
    dot_general x54, matrix products, close_branch(): lax.dot_general(moved.reshape(row_count, channels), conv_weight[index], c...  33.4 us
    ppermute x18, starting transfers between devices, extended(): lax.ppermute(head, axis, [((i + 1) % count, i) for i in range(ends)])  23.1 us
    ppermute x18, waiting for transfers between devices, extended(): lax.ppermute(tail, axis, [(i, (i + 1) % count) for i in range(ends)])  22.7 us
  transfers between devices with their start and end apart: 56, of which 39 were waited for; matrix products, arithmetic and copies ran while one was open for 0% of the time, Pallas kernels for 0%

commit v1 on v0

v1 whole, which is shorter than its diff:
```python
import functools

import jax
import jax.numpy as jnp
from jax import lax
from jax.experimental import pallas as pl
from jax.experimental.pallas import tpu as pltpu
from jax.sharding import PartitionSpec as P

MESH = pl.DeviceIdType.MESH
BF = jnp.bfloat16
F32 = jnp.float32
NX, NY, NLO = 4, 8, 4
CHUNKS = 7
ROWS = 32
NT = (((1,), (1,)), ((), ()))


def kernel(
    x_hbm, pre_hbm, og_hbm, cw_hbm, pw_hbm,
    sg_out, gc_out, gp_out,
    xb, preb, ogb, cw, pw, pre32, gb, gob, planes, sg_in, shifted, grads,
    left, left_last, t_other, t_own, core_in, s_buf, x_in1, x_out, x_in2, r_buf, y_in, f_buf, f_in,
    lsem, psend, precv, rsend, rrecv, osend, orecv, csend, crecv, xsend, xrecv, ysend, yrecv, fsend, frecv,
):
    s = lax.axis_index("section")
    dp = lax.axis_index("dp")
    p = lax.axis_index("space")
    last = lax.axis_size("section") - 1
    core = lax.rem(dp, 2)
    xx = lax.rem(lax.div(dp, 2), NX)
    ylo = lax.div(dp, 2 * NX)
    yy = p * NLO + ylo
    other = 1 - p
    scale = 1.0 / (2 * lax.axis_size("dp"))

    def at_dp(x, y_lo, c):
        return (y_lo * NX + x) * 2 + c

    x_right, x_left = lax.rem(xx + 1, NX), lax.rem(xx + NX - 1, NX)
    x_far = lax.rem(xx + 2, NX)
    partner = {"space": other}
    core_peer = {"dp": at_dp(xx, ylo, 1 - core)}
    right = {"dp": at_dp(x_right, ylo, core)}
    left_dev = {"dp": at_dp(x_left, ylo, core)}

    def y_dev(k):
        t = lax.rem(yy + k, NY)
        return t, {"dp": at_dp(xx, lax.rem(t, NLO), core), "space": lax.div(t, NLO)}

    local = [
        pltpu.make_async_copy(pre_hbm.at[p], preb.at[p], lsem.at[0]),
        pltpu.make_async_copy(og_hbm.at[p], ogb.at[p], lsem.at[1]),
        pltpu.make_async_copy(pw_hbm, pw, lsem.at[2]),
        pltpu.make_async_copy(cw_hbm, cw, lsem.at[3]),
        pltpu.make_async_copy(x_hbm.at[p], xb.at[p], lsem.at[4]),
    ]
    for copy in local:
        copy.start()

    barrier = pltpu.get_barrier_semaphore()

    def greet(device):
        pl.semaphore_signal(barrier, inc=1, device_id=device, device_id_type=MESH)

    count = last + 1
    greet({"section": lax.rem(s + 1, count)})
    greet({"section": lax.rem(s + last, count)})
    greet(core_peer)
    greet(right)
    greet(left_dev)
    for k in range(1, NY):
        greet(y_dev(k)[1])

    pl.semaphore_wait(barrier, 5 + NY - 1)

    def remote(src, dst, ssem, rsem, device):
        return pltpu.make_async_remote_copy(
            src_ref=src, dst_ref=dst, send_sem=ssem, recv_sem=rsem, device_id=device, device_id_type=MESH
        )

    swaps = [
        remote(pre_hbm.at[other], preb.at[p], psend.at[0], precv.at[0], partner),
        remote(og_hbm.at[other], ogb.at[p], psend.at[1], precv.at[1], partner),
        remote(x_hbm.at[other], xb.at[p], psend.at[2], precv.at[2], partner),
    ]
    for copy in swaps:
        copy.start()

    def both(ref):
        pair = jnp.stack([ref[0].astype(F32), ref[1].astype(F32)], axis=1)
        return pair.reshape(128, 256)

    edge = jnp.zeros((3, 3, 16, 256), BF)
    shifted[:, :, 0:16] = edge
    shifted[:, :, 144:160] = edge
    local[0].wait()
    swaps[0].wait()
    pre32[...] = both(preb)
    local[1].wait()
    swaps[1].wait()

    @pl.when(s == last)
    def _():
        gb[...] = both(ogb).astype(BF)

    local[2].wait()

    def lanes():
        v = lax.broadcasted_iota(jnp.int32, (256, 128), 1)
        return v // 16, (v // 8) % 2, v % 8

    def build_left():
        local[4].wait()
        swaps[2].wait()
        xt = both(xb).T
        hid = jnp.maximum(pre32[...], 0.0).T
        lh, ld, lw = lanes()
        slabs = []
        for kd in (-1, 0, 1):
            for kh in (-1, 0, 1):
                for kw in (-1, 0, 1):
                    slabs.append((kd, kh, kw))

        def slab(index):
            kd, kh, kw = slabs[index]
            off = 16 * kh + 8 * kd + kw
            moved = xt if off == 0 else pltpu.roll(xt, (-off) % 128, 1)
            good = None
            for pos, k, top in ((lh, kh, 7), (ld, kd, 1), (lw, kw, 7)):
                if k != 0:
                    ok = pos >= 1 if k < 0 else pos <= top - 1
                    good = ok if good is None else good & ok
            if good is not None:
                moved = jnp.where(good, moved, 0.0)
            return moved.reshape(16, 2, 8, 128)

        zero = jnp.zeros((16, 2, 8, 128), F32)
        for chunk in range(CHUNKS):
            for pair in range(2):
                first = chunk * 4 + pair * 2
                a = slab(first)
                b = slab(first + 1) if first + 1 < 27 else zero
                tile = jnp.concatenate([a, b], axis=2).astype(BF)
                for c in range(2):
                    if chunk < CHUNKS - 1:
                        left[chunk, c, :, 16 * pair : 16 * pair + 16, :] = tile[:, c]
                    else:
                        left_last[c, :, 16 * pair : 16 * pair + 16, 0:128] = tile[:, c]
        h4 = hid.reshape(16, 2, 8, 128)
        tail = jnp.concatenate([zero, h4], axis=2).astype(BF)
        none = jnp.zeros((16, 16, 128), BF)
        for c in range(2):
            left_last[c, :, 0:16, 128:256] = none
            left_last[c, :, 16:32, 128:256] = tail[:, c]

    def open_block():
        g = gb[...]
        gh = lax.dot_general(g, pw[...], NT, preferred_element_type=F32)
        gpb = jnp.where(pre32[...] > 0, gh, 0.0).astype(BF)
        grads[0:128, :] = gpb
        grads[128:256, :] = g
        return gpb

    def close_block():
        gq = grads[0:128, :].astype(F32).reshape(16, 8, 256)
        w = lax.broadcasted_iota(jnp.int32, (16, 8, 256), 1)
        zeros = jnp.zeros((8, 8, 256), F32)
        for kw in (-1, 0, 1):
            if kw == 0:
                sw = gq
            elif kw == 1:
                sw = jnp.where(w >= 1, pltpu.roll(gq, 1, 1), 0.0)
            else:
                sw = jnp.where(w <= 6, pltpu.roll(gq, 7, 1), 0.0)
            s4 = sw.reshape(8, 2, 8, 256)
            for kd in (-1, 0, 1):
                if kd == 0:
                    val = s4
                elif kd == 1:
                    val = jnp.stack([zeros, s4[:, 0]], axis=1)
                else:
                    val = jnp.stack([s4[:, 1], zeros], axis=1)
                shifted[kd + 1, kw + 1, 16:144, :] = val.reshape(128, 256).astype(BF)
        accs = [gb[...].astype(F32), None]
        index = 0
        for kd in (-1, 0, 1):
            for kh in (-1, 0, 1):
                for kw in (-1, 0, 1):
                    rows = shifted[kd + 1, kw + 1, (1 - kh) * 16 : (1 - kh) * 16 + 128, :]
                    term = lax.dot_general(rows, cw[index], NT, preferred_element_type=F32)
                    side = index % 2
                    accs[side] = term if accs[side] is None else accs[side] + term
                    index += 1
        gob[...] = (accs[0] + accs[1]).astype(BF)

    hand = remote(gob, gb, rsend.at[0], rrecv.at[0], {"section": s - 1})

    @pl.when(s < last)
    def _():
        build_left()
        remote(gob, gb, rsend.at[0], rrecv.at[0], {"section": s + 1}).wait_recv()

    open_block()
    local[3].wait()

    @pl.when(s > 0)
    def _():
        close_block()
        hand.start()

    @pl.when(s == last)
    def _():
        build_left()

    back = remote(planes.at[other], sg_in, osend.at[0], orecv.at[0], partner)

    def give_back():
        @pl.when(s == 0)
        def _():
            close_block()

        gin = gob[...].astype(F32).reshape(8, 2, 8, 256)
        planes[0] = gin[:, 0].astype(BF)
        planes[1] = gin[:, 1].astype(BF)
        back.start()

    def product(chunk, c):
        if chunk < CHUNKS - 1:
            lhs = left[chunk, c].reshape(16 * ROWS, 128)
            rhs = grads[0:128, :]
        else:
            lhs = left_last[c].reshape(16 * ROWS, 256)
            rhs = grads[...]
        outs = []
        for part in range(2):
            span = slice(8 * ROWS * part, 8 * ROWS * (part + 1))
            out = jnp.dot(lhs[span], rhs, preferred_element_type=F32) * scale
            outs.append(out.astype(BF).reshape(NLO // 2, NX, ROWS, 256))
        return jnp.concatenate(outs, axis=0)

    core_copies = []
    for chunk in range(CHUNKS):
        t_other[chunk] = product(chunk, 1 - core)
        copy = remote(t_other.at[chunk], core_in.at[chunk], csend.at[chunk], crecv.at[chunk], core_peer)
        copy.start()
        core_copies.append(copy)
        t_own[chunk] = product(chunk, core)

    copies = []
    x1, x2, yc, fc = {}, {}, {}, {}

    def stage1(chunk):
        core_copies[chunk].wait_recv()
        for x in range(NX):
            s_buf[chunk, x] = (
                t_own[chunk, :, x].astype(F32) + core_in[chunk, :, x].astype(F32)
            ).astype(BF)
        far = s_buf.at[chunk, x_far]
        x1[chunk] = [
            remote(far.at[0:2], x_in1.at[chunk, 0], xsend.at[chunk, 0], xrecv.at[chunk, 0], right),
            remote(far.at[2:4], x_in1.at[chunk, 1], xsend.at[chunk, 1], xrecv.at[chunk, 1], left_dev),
        ]
        for copy in x1[chunk]:
            copy.start()

    def stage2(chunk):
        for copy in x1[chunk]:
            copy.wait_recv()
        to_right = s_buf[chunk, x_right]
        to_left = s_buf[chunk, x_left]
        x_out[chunk, 0, 0:2] = (to_right[0:2].astype(F32) + x_in1[chunk, 0].astype(F32)).astype(BF)
        x_out[chunk, 0, 2:4] = to_right[2:4]
        x_out[chunk, 1, 0:2] = to_left[0:2]
        x_out[chunk, 1, 2:4] = (to_left[2:4].astype(F32) + x_in1[chunk, 1].astype(F32)).astype(BF)
        x2[chunk] = [
            remote(x_out.at[chunk, 0], x_in2.at[chunk, 0], xsend.at[chunk, 2], xrecv.at[chunk, 2], right),
            remote(x_out.at[chunk, 1], x_in2.at[chunk, 1], xsend.at[chunk, 3], xrecv.at[chunk, 3], left_dev),
        ]
        for copy in x2[chunk]:
            copy.start()

    def stage3(chunk):
        for copy in x2[chunk]:
            copy.wait_recv()
        r_buf[chunk] = (
            s_buf[chunk, xx].astype(F32) + x_in2[chunk, 0].astype(F32) + x_in2[chunk, 1].astype(F32)
        ).astype(BF).reshape(NLO, 2, ROWS // 2, 256)
        yc[chunk] = []
        for k in range(1, NY):
            t, device = y_dev(k)
            copy = remote(
                r_buf.at[chunk, lax.rem(t, NLO), lax.div(t, NLO)],
                y_in.at[chunk, k - 1], ysend.at[chunk, k - 1], yrecv.at[chunk, k - 1], device,
            )
            copy.start()
            yc[chunk].append(copy)

    def stage4(chunk):
        total = r_buf[chunk, ylo, p].astype(F32)
        for k in range(1, NY):
            yc[chunk][k - 1].wait_recv()
            total = total + y_in[chunk, k - 1].astype(F32)
        f_buf[chunk] = total.astype(BF)
        fc[chunk] = remote(f_buf.at[chunk], f_in.at[chunk], fsend.at[chunk], frecv.at[chunk], partner)
        fc[chunk].start()

    def stage5(chunk):
        fc[chunk].wait_recv()
        mine = f_buf[chunk].astype(F32).reshape(2, 8, 256)
        theirs = f_in[chunk].astype(F32).reshape(2, 8, 256)
        low = jnp.where(p == 0, mine, theirs)
        high = jnp.where(p == 0, theirs, mine)
        gc_out[4 * chunk : 4 * chunk + 2] = low
        if chunk < CHUNKS - 1:
            gc_out[4 * chunk + 2 : 4 * chunk + 4] = high
        else:
            gc_out[4 * chunk + 2] = high[0]
            gp_out[...] = high[1]

    for chunk in range(CHUNKS):
        stage1(chunk)
    give_back()
    lags = ((stage2, 0), (stage3, 1), (stage4, 3), (stage5, 5))
    for t in range(CHUNKS + 5):
        for stage, lag in lags:
            if 0 <= t - lag < CHUNKS:
                stage(t - lag)

    back.wait_recv()
    sg_out[pl.ds(p, 1)] = planes[pl.ds(p, 1)]
    sg_out[pl.ds(other, 1)] = sg_in[...][None]

    back.wait_send()

    @pl.when(s > 0)
    def _():
        hand.wait_send()

    for chunk in range(CHUNKS):
        core_copies[chunk].wait_send()
        for copy in x1[chunk] + x2[chunk] + yc[chunk]:
            copy.wait_send()
        fc[chunk].wait_send()


def emit(a_in, b_in, c_in, a_out, b_out, c_out):
    a_out[...] = a_in[...]
    b_out[...] = b_in[...]
    c_out[...] = c_in[...]


def shards(inputs, preacts, out_grad, conv_w, proj_w):
    plane = (8, 8, 256)
    args = (
        inputs.reshape((2,) + plane),
        preacts.reshape((2,) + plane),
        out_grad.reshape((2,) + plane),
        conv_w.reshape(27, 256, 256),
        proj_w.reshape(256, 256),
    )
    half = ROWS // 2
    dma = pltpu.SemaphoreType.DMA
    vm = pltpu.VMEM
    scratch = [
        vm((2,) + plane, BF),
        vm((2,) + plane, BF),
        vm((2,) + plane, BF),
        vm((27, 256, 256), BF),
        vm((256, 256), BF),
        vm((128, 256), F32),
        vm((128, 256), BF),
        vm((128, 256), BF),
        vm((2,) + plane, BF),
        vm(plane, BF),
        vm((3, 3, 160, 256), BF),
        vm((256, 256), BF),
        vm((CHUNKS - 1, 2, 16, ROWS, 128), BF),
        vm((2, 16, ROWS, 256), BF),
        vm((CHUNKS, NLO, NX, ROWS, 256), BF),
        vm((CHUNKS, NLO, NX, ROWS, 256), BF),
        vm((CHUNKS, NLO, NX, ROWS, 256), BF),
        vm((CHUNKS, NX, NLO, ROWS, 256), BF),
        vm((CHUNKS, 2, 2, ROWS, 256), BF),
        vm((CHUNKS, 2, NLO, ROWS, 256), BF),
        vm((CHUNKS, 2, NLO, ROWS, 256), BF),
        vm((CHUNKS, NLO, 2, half, 256), BF),
        vm((CHUNKS, NY - 1, half, 256), BF),
        vm((CHUNKS, half, 256), BF),
        vm((CHUNKS, half, 256), BF),
        dma((5,)),
        dma((3,)),
        dma((3,)),
        dma((1,)),
        dma((1,)),
        dma((1,)),
        dma((1,)),
        dma((CHUNKS,)),
        dma((CHUNKS,)),
        dma((CHUNKS, 4)),
        dma((CHUNKS, 4)),
        dma((CHUNKS, NY - 1)),
        dma((CHUNKS, NY - 1)),
        dma((CHUNKS,)),
        dma((CHUNKS,)),
    ]
    sg, gc, gp = pl.pallas_call(
        kernel,
        out_shape=(
            jax.ShapeDtypeStruct((2,) + plane, BF),
            jax.ShapeDtypeStruct((27, 8, 256), F32),
            jax.ShapeDtypeStruct((8, 256), F32),
        ),
        in_specs=[pl.BlockSpec(memory_space=pl.ANY)] * 5,
        out_specs=(pl.BlockSpec(memory_space=pltpu.VMEM),) * 3,
        scratch_shapes=scratch,
        compiler_params=pltpu.CompilerParams(
            collective_id=0, has_side_effects=True, vmem_limit_bytes=60 * 1024 * 1024
        ),
        name="relay",
    )(*args)
    sg, gc, gp = pl.pallas_call(
        emit,
        out_shape=tuple(jax.ShapeDtypeStruct(a.shape, a.dtype) for a in (sg, gc, gp)),
        name="emit",
    )(sg, gc, gp)
    return (
        sg.reshape(1, 2, 1, 1, 8, 8, 256),
        jnp.transpose(gc, (1, 0, 2))[None],
        gp[None],
    )


def solution(mesh):
    placed = (
        P("section", None, "dp", "space", None, None, None),
        P("section", None, "dp", "space", None, None, None),
        P(None, "dp", "space", None, None, None),
        P("section", None, None, None),
        P("section", None, None),
    )
    return jax.shard_map(
        shards,
        mesh=mesh,
        in_specs=placed,
        out_specs=(
            P("section", None, "dp", "space", None, None, None),
            P("section", "dp", None, None),
            P("section", "dp", None),
        ),
        check_vma=False,
    )
```

time: 1050 us -> 140 us (0.13)
  waiting for transfers between devices: 736 us -> 0 us
  starting transfers between devices: 187 us -> 0 us
  Pallas kernels: 0 us -> 137 us
  local copies, waits for them, and re-layouts: 45.7 us -> 0 us
  matrix products: 38.5 us -> 0 us
  other arithmetic: 16.4 us -> 0 us
  between operations: 14.1 us -> 0.64 us
    ppermute x53 -> x0, waiting for transfers between devices: 353 us -> none  [the longest x17 323 us: passed_along(): return lax.ppermute(block, axis, route)]
    reduce_scatter x2 -> x0, waiting for transfers between devices: 336 us -> none  [the longest x1 181 us: shards(): lax.psum_scatter(conv_full.astype(jnp.bfloat16), 'dp', scatter_dimension=...]
    ppermute x53 -> x0, starting transfers between devices: 187 us -> none  [the longest x18 142 us: extended(): lax.ppermute(tail, axis, [(i, (i + 1) % count) for i in range(ends)])]
    pallas_call x0 -> x2, Pallas kernels: none -> 137 us  [the longest x1 136 us: shards(): pl.pallas_call(kernel, out_shape=(jax.ShapeDtypeStruct((2,) + plane, BF),...]
    psum x1 -> x0, waiting for transfers between devices: 47.5 us -> none  [shards(): lax.psum(conv_shard.astype(jnp.bfloat16), 'space').astype(jnp.float32)]
    dot_general x58 -> x0, matrix products: 38.5 us -> none  [the longest x54 33.4 us: close_branch(): lax.dot_general(moved.reshape(row_count, channels), conv_weight[index], c...]
    another operation x36 -> x0, local copies, waits for them, and re-layouts: 25.5 us -> none
    concatenate x18 -> x0, other arithmetic: 14.1 us -> none  [extended(): jnp.concatenate([lax.ppermute(tail, axis, [(i, (i + 1) % count) for i in...]
  transfers between devices with their start and end apart: 56 -> 0, of which waited for: 39 -> 0; matrix products, arithmetic and copies ran while one was open for 0% -> 0% of each run, Pallas kernels for 0% -> 0%
where the time goes in v1:
time: 140 us; the launch traced here: 138 us
  Pallas kernels  137 us (98%)
    pallas_call x1, Pallas kernels, shards(): pl.pallas_call(kernel, out_shape=(jax.ShapeDtypeStruct((2,) + plane, BF),...  136 us

profile of v1, /device:TPU:1, one launch (start us, length us, event | category | flops | bytes accessed | tf_op | source)
XLA Modules:
  0.0 137.9 jit_solution(1180197164333641307)
XLA Ops:
  0.6 135.5 %relay.1 = (bf16[2,8,8,256]{3,2,1,0:T(8,128)(2,1)}, f32[27,8,256]{2,1,0:T(8,128)}, f32[8,256]{1,0:T(8,128)}) custom-call(bf16[2,8,8,256]{3,2,1,0:T(8,128)(2,1)} %bitcast.14, bf16[2,8,8,256]{3,2,1,0:T(8,128)(2,1)} %bitcast.15, bf16[2,8,8,256]{3,2,1,0:T(8,128)(2,1)} %bitcast.16, bf16[27,256,256]{2,1,0:T(8,128)(2,1)} %bitcast.12, bf16[256,256]{1,0:T(8,128)(2,1)} %bitcast.13), custom_call_target="tpu_custom_call" | custom-call | tf_op jit(solution)/shard_map/relay/pallas_call | solution.py:407
  136.2 1.7 %emit.1 = (bf16[2,8,8,256]{3,2,1,0:T(8,128)(2,1)}, f32[27,8,256]{2,1,0:T(8,128)}, f32[8,256]{1,0:T(8,128)}) custom-call(bf16[2,8,8,256]{3,2,1,0:T(8,128)(2,1)} %get-tuple-element.9.a_in, f32[27,8,256]{2,1,0:T(8,128)} %get-tuple-element.10.b_in, f32[8,256]{1,0:T(8,128)} %get-tuple-element.11.c_in), custom_call_target="tpu_custom_call" | custom-call | tf_op jit(solution)/shard_map/emit/pallas_call | solution.py:422

commit v2 on v1

--- a/solution.py
+++ b/solution.py
@@ -19,8 +19,8 @@
 def kernel(
     x_hbm, pre_hbm, og_hbm, cw_hbm, pw_hbm,
     sg_out, gc_out, gp_out,
-    xb, preb, ogb, cw, pw, pre32, gb, gob, planes, sg_in, shifted, grads,
-    left, left_last, t_other, t_own, core_in, s_buf, x_in1, x_out, x_in2, r_buf, y_in, f_buf, f_in,
+    xb, preb, ogb, cw, pw, pre32, gb, gob, planes, sg_in, shifted, grads, cwt,
+    left, left_last, t_other, core_in, s_buf, x_in1, x_out, x_in2, r_buf, y_in, y_last, f_buf, f_in,
     lsem, psend, precv, rsend, rrecv, osend, orecv, csend, crecv, xsend, xrecv, ysend, yrecv, fsend, frecv,
 ):
     s = lax.axis_index("section")
@@ -40,7 +40,10 @@
     x_right, x_left = lax.rem(xx + 1, NX), lax.rem(xx + NX - 1, NX)
     x_far = lax.rem(xx + 2, NX)
     partner = {"space": other}
-    core_peer = {"dp": at_dp(xx, ylo, 1 - core)}
+    odd = lax.rem(s, 2)
+    twin = at_dp(xx, ylo, 1 - core)
+    core_peer = {"dp": twin}
+    corner = {"dp": twin, "space": other}
     right = {"dp": at_dp(x_right, ylo, core)}
     left_dev = {"dp": at_dp(x_left, ylo, core)}
 
@@ -48,15 +51,12 @@
         t = lax.rem(yy + k, NY)
         return t, {"dp": at_dp(xx, lax.rem(t, NLO), core), "space": lax.div(t, NLO)}
 
-    local = [
-        pltpu.make_async_copy(pre_hbm.at[p], preb.at[p], lsem.at[0]),
-        pltpu.make_async_copy(og_hbm.at[p], ogb.at[p], lsem.at[1]),
-        pltpu.make_async_copy(pw_hbm, pw, lsem.at[2]),
-        pltpu.make_async_copy(cw_hbm, cw, lsem.at[3]),
-        pltpu.make_async_copy(x_hbm.at[p], xb.at[p], lsem.at[4]),
-    ]
-    for copy in local:
+    def fetch(src, dst, sem):
+        copy = pltpu.make_async_copy(src, dst, sem)
         copy.start()
+        return copy
+
+    weights = [fetch(pw_hbm, pw, lsem.at[2]), fetch(cw_hbm, cw, lsem.at[3])]
 
     barrier = pltpu.get_barrier_semaphore()
 
@@ -64,28 +64,58 @@
         pl.semaphore_signal(barrier, inc=1, device_id=device, device_id_type=MESH)
 
     count = last + 1
-    greet({"section": lax.rem(s + 1, count)})
-    greet({"section": lax.rem(s + last, count)})
+    greet({"section": lax.rem(s + 1, count), "dp": twin})
+    greet({"section": lax.rem(s + last, count), "dp": twin})
     greet(core_peer)
+    greet(corner)
     greet(right)
     greet(left_dev)
     for k in range(1, NY):
         greet(y_dev(k)[1])
 
-    pl.semaphore_wait(barrier, 5 + NY - 1)
+    pl.semaphore_wait(barrier, 6 + NY - 1)
 
     def remote(src, dst, ssem, rsem, device):
         return pltpu.make_async_remote_copy(
             src_ref=src, dst_ref=dst, send_sem=ssem, recv_sem=rsem, device_id=device, device_id_type=MESH
         )
 
-    swaps = [
-        remote(pre_hbm.at[other], preb.at[p], psend.at[0], precv.at[0], partner),
-        remote(og_hbm.at[other], ogb.at[p], psend.at[1], precv.at[1], partner),
-        remote(x_hbm.at[other], xb.at[p], psend.at[2], precv.at[2], partner),
-    ]
-    for copy in swaps:
-        copy.start()
+    sources = ((pre_hbm, preb), (og_hbm, ogb), (x_hbm, xb))
+
+    def own_local(n):
+        src, dst = sources[n]
+        return pltpu.make_async_copy(src.at[p], dst.at[p], lsem.at[4 + n])
+
+    def own_remote(n):
+        src, dst = sources[n]
+        return remote(src.at[p], dst.at[p], psend.at[3 + n], precv.at[3 + n], core_peer)
+
+    def swap(n, device):
+        src, dst = sources[n]
+        return remote(src.at[other], dst.at[p], psend.at[n], precv.at[n], device)
+
+    @pl.when(odd == 0)
+    def _():
+        for n in range(3):
+            swap(n, partner).start()
+            own_local(n).start()
+
+    @pl.when(odd == 1)
+    def _():
+        for n in range(3):
+            swap(n, corner).start()
+            own_remote(n).start()
+
+    def landed(n):
+        swap(n, partner).wait_recv()
+
+        @pl.when(odd == 0)
+        def _():
+            own_local(n).wait()
+
+        @pl.when(odd == 1)
+        def _():
+            own_remote(n).wait_recv()
 
     def both(ref):
         pair = jnp.stack([ref[0].astype(F32), ref[1].astype(F32)], axis=1)
@@ -94,25 +124,22 @@
     edge = jnp.zeros((3, 3, 16, 256), BF)
     shifted[:, :, 0:16] = edge
     shifted[:, :, 144:160] = edge
-    local[0].wait()
-    swaps[0].wait()
+    landed(0)
     pre32[...] = both(preb)
-    local[1].wait()
-    swaps[1].wait()
+    landed(1)
 
     @pl.when(s == last)
     def _():
         gb[...] = both(ogb).astype(BF)
 
-    local[2].wait()
+    weights[0].wait()
 
     def lanes():
         v = lax.broadcasted_iota(jnp.int32, (256, 128), 1)
         return v // 16, (v // 8) % 2, v % 8
 
     def build_left():
-        local[4].wait()
-        swaps[2].wait()
+        landed(2)
         xt = both(xb).T
         hid = jnp.maximum(pre32[...], 0.0).T
         lh, ld, lw = lanes()
@@ -162,7 +189,12 @@
         grads[128:256, :] = g
         return gpb
 
-    def close_block():
+    def turn_weights():
+        @pl.loop(0, 27)
+        def _(k):
+            cwt[k] = cw[k].T
+
+    def close_block(turned):
         gq = grads[0:128, :].astype(F32).reshape(16, 8, 256)
         w = lax.broadcasted_iota(jnp.int32, (16, 8, 256), 1)
         zeros = jnp.zeros((8, 8, 256), F32)
@@ -188,42 +220,71 @@
             for kh in (-1, 0, 1):
                 for kw in (-1, 0, 1):
                     rows = shifted[kd + 1, kw + 1, (1 - kh) * 16 : (1 - kh) * 16 + 128, :]
-                    term = lax.dot_general(rows, cw[index], NT, preferred_element_type=F32)
+                    if turned:
+                        term = jnp.dot(rows, cwt[index], preferred_element_type=F32)
+                    else:
+                        term = lax.dot_general(rows, cw[index], NT, preferred_element_type=F32)
                     side = index % 2
                     accs[side] = term if accs[side] is None else accs[side] + term
                     index += 1
         gob[...] = (accs[0] + accs[1]).astype(BF)
 
-    hand = remote(gob, gb, rsend.at[0], rrecv.at[0], {"section": s - 1})
+    hand = remote(gob, gb, rsend.at[0], rrecv.at[0], {"section": s - 1, "dp": twin})
+
+    early = (s == last) & (core == 0)
+    weights[1].wait()
 
     @pl.when(s < last)
     def _():
+        turn_weights()
+
+    @pl.when(jnp.logical_not(early))
+    def _():
         build_left()
-        remote(gob, gb, rsend.at[0], rrecv.at[0], {"section": s + 1}).wait_recv()
+
+    @pl.when(s < last)
+    def _():
+        remote(gob, gb, rsend.at[0], rrecv.at[0], {"section": s + 1, "dp": twin}).wait_recv()
 
     open_block()
-    local[3].wait()
-
-    @pl.when(s > 0)
-    def _():
-        close_block()
+
+    @pl.when(s == last)
+    def _():
+        close_block(False)
         hand.start()
 
-    @pl.when(s == last)
+    @pl.when((s > 0) & (s < last))
+    def _():
+        close_block(True)
+        hand.start()
+
+    @pl.when(early)
     def _():
         build_left()
 
-    back = remote(planes.at[other], sg_in, osend.at[0], orecv.at[0], partner)
+    def back(device):
+        return remote(planes.at[other], sg_in.at[p], osend.at[0], orecv.at[0], device)
+
+    def back_own():
+        return remote(planes.at[p], sg_in.at[p], osend.at[1], orecv.at[1], core_peer)
 
     def give_back():
         @pl.when(s == 0)
         def _():
-            close_block()
+            close_block(True)
 
         gin = gob[...].astype(F32).reshape(8, 2, 8, 256)
         planes[0] = gin[:, 0].astype(BF)
         planes[1] = gin[:, 1].astype(BF)
-        back.start()
+
+        @pl.when(odd == 0)
+        def _():
+            back(partner).start()
+
+        @pl.when(odd == 1)
+        def _():
+            back(corner).start()
+            back_own().start()
 
     def product(chunk, c):
         if chunk < CHUNKS - 1:
@@ -236,26 +297,27 @@
         for part in range(2):
             span = slice(8 * ROWS * part, 8 * ROWS * (part + 1))
             out = jnp.dot(lhs[span], rhs, preferred_element_type=F32) * scale
-            outs.append(out.astype(BF).reshape(NLO // 2, NX, ROWS, 256))
-        return jnp.concatenate(outs, axis=0)
+            outs.append(out.reshape(NLO // 2, NX, ROWS, 256))
+        return outs
 
     core_copies = []
     for chunk in range(CHUNKS):
-        t_other[chunk] = product(chunk, 1 - core)
+        for part, out in enumerate(product(chunk, 1 - core)):
+            t_other[chunk, 2 * part : 2 * part + 2] = out.astype(BF)
         copy = remote(t_other.at[chunk], core_in.at[chunk], csend.at[chunk], crecv.at[chunk], core_peer)
         copy.start()
         core_copies.append(copy)
-        t_own[chunk] = product(chunk, core)
-
-    copies = []
+
     x1, x2, yc, fc = {}, {}, {}, {}
 
     def stage1(chunk):
+        own = product(chunk, core)
         core_copies[chunk].wait_recv()
-        for x in range(NX):
-            s_buf[chunk, x] = (
-                t_own[chunk, :, x].astype(F32) + core_in[chunk, :, x].astype(F32)
-            ).astype(BF)
+        for part in range(2):
+            for x in range(NX):
+                s_buf[chunk, x, 2 * part : 2 * part + 2] = (
+                    own[part][:, x] + core_in[chunk, 2 * part : 2 * part + 2, x].astype(F32)
+                ).astype(BF)
         far = s_buf.at[chunk, x_far]
         x1[chunk] = [
             remote(far.at[0:2], x_in1.at[chunk, 0], xsend.at[chunk, 0], xrecv.at[chunk, 0], right),
@@ -289,14 +351,28 @@
         yc[chunk] = []
         for k in range(1, NY):
             t, device = y_dev(k)
+            if chunk == CHUNKS - 1:
+                src, dst = r_buf.at[chunk, lax.rem(t, NLO)], y_last.at[yy]
+            else:
+                src, dst = r_buf.at[chunk, lax.rem(t, NLO), lax.div(t, NLO)], y_in.at[chunk, k - 1]
             copy = remote(
-                r_buf.at[chunk, lax.rem(t, NLO), lax.div(t, NLO)],
-                y_in.at[chunk, k - 1], ysend.at[chunk, k - 1], yrecv.at[chunk, k - 1], device,
+                src, dst, ysend.at[chunk, k - 1], yrecv.at[chunk, k - 1], device,
             )
             copy.start()
             yc[chunk].append(copy)
 
     def stage4(chunk):
+        if chunk == CHUNKS - 1:
+            y_last[pl.ds(yy, 1)] = r_buf[chunk, pl.ds(ylo, 1)]
+            for copy in yc[chunk]:
+                copy.wait_recv()
+            total = y_last[0].astype(F32)
+            for t in range(1, NY):
+                total = total + y_last[t].astype(F32)
+            total = total.reshape(4, 8, 256)
+            gc_out[4 * chunk : 4 * chunk + 3] = total[0:3]
+            gp_out[...] = total[3]
+            return
         total = r_buf[chunk, ylo, p].astype(F32)
         for k in range(1, NY):
             yc[chunk][k - 1].wait_recv()
@@ -312,11 +388,7 @@
         low = jnp.where(p == 0, mine, theirs)
         high = jnp.where(p == 0, theirs, mine)
         gc_out[4 * chunk : 4 * chunk + 2] = low
-        if chunk < CHUNKS - 1:
-            gc_out[4 * chunk + 2 : 4 * chunk + 4] = high
-        else:
-            gc_out[4 * chunk + 2] = high[0]
-            gp_out[...] = high[1]
+        gc_out[4 * chunk + 2 : 4 * chunk + 4] = high
 
     for chunk in range(CHUNKS):
         stage1(chunk)
@@ -324,14 +396,27 @@
     lags = ((stage2, 0), (stage3, 1), (stage4, 3), (stage5, 5))
     for t in range(CHUNKS + 5):
         for stage, lag in lags:
-            if 0 <= t - lag < CHUNKS:
+            if 0 <= t - lag < CHUNKS - (lag == 5):
                 stage(t - lag)
 
-    back.wait_recv()
-    sg_out[pl.ds(p, 1)] = planes[pl.ds(p, 1)]
-    sg_out[pl.ds(other, 1)] = sg_in[...][None]
-
-    back.wait_send()
+    back(partner).wait_recv()
+    sg_out[pl.ds(other, 1)] = sg_in[pl.ds(other, 1)]
+
+    @pl.when(odd == 0)
+    def _():
+        sg_out[pl.ds(p, 1)] = planes[pl.ds(p, 1)]
+
+    @pl.when(odd == 1)
+    def _():
+        back_own().wait_recv()
+        sg_out[pl.ds(p, 1)] = sg_in[pl.ds(p, 1)]
+        back_own().wait_send()
+        for n in range(3):
+            own_remote(n).wait_send()
+
+    back(partner).wait_send()
+    for n in range(3):
+        swap(n, partner).wait_send()
 
     @pl.when(s > 0)
     def _():
@@ -341,7 +426,8 @@
         core_copies[chunk].wait_send()
         for copy in x1[chunk] + x2[chunk] + yc[chunk]:
             copy.wait_send()
-        fc[chunk].wait_send()
+        if chunk in fc:
+            fc[chunk].wait_send()
 
 
 def emit(a_in, b_in, c_in, a_out, b_out, c_out):
@@ -372,12 +458,12 @@
         vm((128, 256), BF),
         vm((128, 256), BF),
         vm((2,) + plane, BF),
-        vm(plane, BF),
+        vm((2,) + plane, BF),
         vm((3, 3, 160, 256), BF),
         vm((256, 256), BF),
+        vm((27, 256, 256), BF),
         vm((CHUNKS - 1, 2, 16, ROWS, 128), BF),
         vm((2, 16, ROWS, 256), BF),
-        vm((CHUNKS, NLO, NX, ROWS, 256), BF),
         vm((CHUNKS, NLO, NX, ROWS, 256), BF),
         vm((CHUNKS, NLO, NX, ROWS, 256), BF),
         vm((CHUNKS, NX, NLO, ROWS, 256), BF),
@@ -386,15 +472,16 @@
         vm((CHUNKS, 2, NLO, ROWS, 256), BF),
         vm((CHUNKS, NLO, 2, half, 256), BF),
         vm((CHUNKS, NY - 1, half, 256), BF),
+        vm((NY, 2, half, 256), BF),
         vm((CHUNKS, half, 256), BF),
         vm((CHUNKS, half, 256), BF),
-        dma((5,)),
-        dma((3,)),
-        dma((3,)),
+        dma((7,)),
+        dma((6,)),
+        dma((6,)),
         dma((1,)),
         dma((1,)),
-        dma((1,)),
-        dma((1,)),
+        dma((2,)),
+        dma((2,)),
         dma((CHUNKS,)),
         dma((CHUNKS,)),
         dma((CHUNKS, 4)),

time: 140 us -> 127 us (0.907)
  the two profiles are of different devices: /device:TPU:1 before, /device:TPU:18 now
where the time goes in v2:
time: 127 us
  Pallas kernels  126 us (99%)
    pallas_call x1, Pallas kernels, shards(): pl.pallas_call(kernel, out_shape=(jax.ShapeDtypeStruct((2,) + plane, BF),...  124 us

profile of v2, /device:TPU:18, one launch (start us, length us, event | category | flops | bytes accessed | tf_op | source)
XLA Modules:
  0.0 126.8 jit_solution(13913457174076119660)
XLA Ops:
  0.6 124.5 %relay.1 = (bf16[2,8,8,256]{3,2,1,0:T(8,128)(2,1)}, f32[27,8,256]{2,1,0:T(8,128)}, f32[8,256]{1,0:T(8,128)}) custom-call(bf16[2,8,8,256]{3,2,1,0:T(8,128)(2,1)} %bitcast.14, bf16[2,8,8,256]{3,2,1,0:T(8,128)(2,1)} %bitcast.15, bf16[2,8,8,256]{3,2,1,0:T(8,128)(2,1)} %bitcast.16, bf16[27,256,256]{2,1,0:T(8,128)(2,1)} %bitcast.12, bf16[256,256]{1,0:T(8,128)(2,1)} %bitcast.13), custom_call_target="tpu_custom_call" | custom-call | tf_op jit(solution)/shard_map/relay/pallas_call | solution.py:494
  125.1 1.7 %emit.1 = (bf16[2,8,8,256]{3,2,1,0:T(8,128)(2,1)}, f32[27,8,256]{2,1,0:T(8,128)}, f32[8,256]{1,0:T(8,128)}) custom-call(bf16[2,8,8,256]{3,2,1,0:T(8,128)(2,1)} %get-tuple-element.9.a_in, f32[27,8,256]{2,1,0:T(8,128)} %get-tuple-element.10.b_in, f32[8,256]{1,0:T(8,128)} %get-tuple-element.11.c_in), custom_call_target="tpu_custom_call" | custom-call | tf_op jit(solution)/shard_map/emit/pallas_call | solution.py:509

commit v3 on v2

--- a/solution.py
+++ b/solution.py
@@ -348,8 +348,8 @@
         r_buf[chunk] = (
             s_buf[chunk, xx].astype(F32) + x_in2[chunk, 0].astype(F32) + x_in2[chunk, 1].astype(F32)
         ).astype(BF).reshape(NLO, 2, ROWS // 2, 256)
-        yc[chunk] = []
-        for k in range(1, NY):
+        yc[chunk] = {}
+        for k in (4, 3, 5, 2, 6, 1, 7):
             t, device = y_dev(k)
             if chunk == CHUNKS - 1:
                 src, dst = r_buf.at[chunk, lax.rem(t, NLO)], y_last.at[yy]
@@ -359,13 +359,13 @@
                 src, dst, ysend.at[chunk, k - 1], yrecv.at[chunk, k - 1], device,
             )
             copy.start()
-            yc[chunk].append(copy)
+            yc[chunk][k] = copy
 
     def stage4(chunk):
         if chunk == CHUNKS - 1:
             y_last[pl.ds(yy, 1)] = r_buf[chunk, pl.ds(ylo, 1)]
-            for copy in yc[chunk]:
-                copy.wait_recv()
+            for k in range(1, NY):
+                yc[chunk][k].wait_recv()
             total = y_last[0].astype(F32)
             for t in range(1, NY):
                 total = total + y_last[t].astype(F32)
@@ -375,7 +375,7 @@
             return
         total = r_buf[chunk, ylo, p].astype(F32)
         for k in range(1, NY):
-            yc[chunk][k - 1].wait_recv()
+            yc[chunk][k].wait_recv()
             total = total + y_in[chunk, k - 1].astype(F32)
         f_buf[chunk] = total.astype(BF)
         fc[chunk] = remote(f_buf.at[chunk], f_in.at[chunk], fsend.at[chunk], frecv.at[chunk], partner)
@@ -390,13 +390,12 @@
         gc_out[4 * chunk : 4 * chunk + 2] = low
         gc_out[4 * chunk + 2 : 4 * chunk + 4] = high
 
-    for chunk in range(CHUNKS):
-        stage1(chunk)
-    give_back()
-    lags = ((stage2, 0), (stage3, 1), (stage4, 3), (stage5, 5))
-    for t in range(CHUNKS + 5):
+    lags = ((stage1, 0), (stage2, 2), (stage3, 4), (stage4, 6), (stage5, 8))
+    for t in range(CHUNKS + 8):
+        if t == 2:
+            give_back()
         for stage, lag in lags:
-            if 0 <= t - lag < CHUNKS - (lag == 5):
+            if 0 <= t - lag < CHUNKS - (lag == 8):
                 stage(t - lag)
 
     back(partner).wait_recv()
@@ -424,7 +423,7 @@
 
     for chunk in range(CHUNKS):
         core_copies[chunk].wait_send()
-        for copy in x1[chunk] + x2[chunk] + yc[chunk]:
+        for copy in x1[chunk] + x2[chunk] + [yc[chunk][k] for k in range(1, NY)]:
             copy.wait_send()
         if chunk in fc:
             fc[chunk].wait_send()

time: 127 us -> 124 us (0.976)
  the two profiles are of different devices: /device:TPU:18 before, /device:TPU:2 now
where the time goes in v3:
time: 124 us
  Pallas kernels  123 us (99%)
    pallas_call x1, Pallas kernels, shards(): pl.pallas_call(kernel, out_shape=(jax.ShapeDtypeStruct((2,) + plane, BF),...  122 us

profile of v3, /device:TPU:2, one launch (start us, length us, event | category | flops | bytes accessed | tf_op | source)
XLA Modules:
  0.0 123.8 jit_solution(2003344824421672796)
XLA Ops:
  0.6 121.5 %relay.1 = (bf16[2,8,8,256]{3,2,1,0:T(8,128)(2,1)}, f32[27,8,256]{2,1,0:T(8,128)}, f32[8,256]{1,0:T(8,128)}) custom-call(bf16[2,8,8,256]{3,2,1,0:T(8,128)(2,1)} %bitcast.14, bf16[2,8,8,256]{3,2,1,0:T(8,128)(2,1)} %bitcast.15, bf16[2,8,8,256]{3,2,1,0:T(8,128)(2,1)} %bitcast.16, bf16[27,256,256]{2,1,0:T(8,128)(2,1)} %bitcast.12, bf16[256,256]{1,0:T(8,128)(2,1)} %bitcast.13), custom_call_target="tpu_custom_call" | custom-call | tf_op jit(solution)/shard_map/relay/pallas_call | solution.py:493
  122.2 1.7 %emit.1 = (bf16[2,8,8,256]{3,2,1,0:T(8,128)(2,1)}, f32[27,8,256]{2,1,0:T(8,128)}, f32[8,256]{1,0:T(8,128)}) custom-call(bf16[2,8,8,256]{3,2,1,0:T(8,128)(2,1)} %get-tuple-element.9.a_in, f32[27,8,256]{2,1,0:T(8,128)} %get-tuple-element.10.b_in, f32[8,256]{1,0:T(8,128)} %get-tuple-element.11.c_in), custom_call_target="tpu_custom_call" | custom-call | tf_op jit(solution)/shard_map/emit/pallas_call | solution.py:508
